TPU v7x, 256 devices: a whole 4x4x8 slice. The times are simulated.
256 devices in a mesh: blk: 32 (over y, z), row: 8 (over x, core).
Axes of the slice: x: 4, y: 4, z: 8, core: 2. Of those that a mesh axis runs over, the one named last changes fastest.
Arguments:
- far_kernel: bfloat16 [256, 8, 512, 512], P('blk', None, 'row'), may hold values from -0.25 to 0.25
- near_kernel: bfloat16 [256, 2, 512, 512], P('blk', None, 'row'), may hold values from -0.25 to 0.25
- samples: bfloat16 [256, 512, 128], P('blk'), may hold values from -18 to 18
- far_target: int32 [256, 8], P('blk'), may hold values from 0 to 255, as said below
Outputs:
- basis_out: float32 [256, 512, 128], P('blk', 'row')
- coupling: float32 [256, 8, 128, 128], P('blk', None, 'row')
- parent_samples: float32 [128, 256, 128], P('blk', 'row')
Inputs may be any that keep to these rules, and one draw needn't show every extreme that they name: `far_target`: each row names 8 different target clusters; among the far blocks of the source clusters of one index of blk (rows 8 * g to 8 * g + 7), at most 4 name targets of any one index of blk (clusters 8 * h to 8 * h + 7), and exactly 4 for some such index.
All inputs are finite; a program needn't handle non-finite values.
Results may differ from a plain program's by a relative error of at most 0.02.
Values may be sent and summed in bfloat16 or wider, within the bound.
No kernel may reach another device: no remote copies, remote signals or barrier semaphores. Data moves between devices by JAX's collectives and lax.ppermute only.
A program may use at most 64 MiB of HBM per device.

v0:
```python
import jax
import jax.numpy as jnp
from jax import lax
from jax.sharding import PartitionSpec as P

ITERS = 12


def inverse_root(gram_mat, full_width):
    highest = lax.Precision.HIGHEST
    sample_cols = gram_mat.shape[-1]
    identity = jnp.eye(sample_cols, dtype=jnp.float32)
    mean_sq = jnp.trace(gram_mat, axis1=1, axis2=2) / (full_width * sample_cols) + 1e-06
    level_mat = gram_mat / (full_width * sample_cols * mean_sq)[:, None, None]
    root_mat = jnp.broadcast_to(identity, gram_mat.shape)
    for sweep_index in range(ITERS):
        step_mat = 1.5 * identity - 0.5 * jnp.matmul(root_mat, level_mat, precision=highest)
        level_mat = jnp.matmul(level_mat, step_mat, precision=highest)
        root_mat = jnp.matmul(step_mat, root_mat, precision=highest)
    return root_mat / jnp.sqrt(sample_cols * mean_sq)[:, None, None]


def per_device(far_kernel, near_kernel, samples, far_target):
    highest = lax.Precision.HIGHEST
    local_count, far_count, row_count, full_width = far_kernel.shape
    sample_cols = samples.shape[2]
    row_offset = lax.axis_index("row") * row_count
    targets = far_target.reshape(local_count * far_count)
    flat_width = row_count * sample_cols
    products = jnp.einsum("cfrw,cws->cfrs", far_kernel, samples, preferred_element_type=jnp.float32)
    products = products.astype(jnp.bfloat16).reshape(local_count * far_count, flat_width)
    target_ids = lax.iota(jnp.int32, local_count * lax.axis_size("blk"))
    onehot = (target_ids[:, None] == targets[None, :]).astype(jnp.bfloat16)
    far_sketch = lax.psum_scatter(
        jnp.dot(onehot, products, preferred_element_type=jnp.float32).astype(jnp.bfloat16),
        "blk",
        scatter_dimension=0,
        tiled=True,
    ).astype(jnp.float32)
    sibling = samples.reshape(local_count // 2, 2, full_width, sample_cols)[:, ::-1].reshape(
        local_count, full_width, sample_cols
    )
    paired = jnp.stack([samples, sibling], axis=1)
    near_sum = jnp.einsum("ckrw,ckws->crs", near_kernel, paired, preferred_element_type=jnp.float32)
    sketch = far_sketch.reshape(local_count, row_count, sample_cols) - near_sum
    gram_part = jnp.einsum("crs,crt->cst", sketch, sketch, precision=highest)
    gram_mat = lax.psum(gram_part, "row")
    root_mat = inverse_root(gram_mat, full_width)
    basis_out = jnp.einsum("crs,cst->crt", sketch, root_mat, precision=highest)
    basis_half = basis_out.astype(jnp.bfloat16)
    start_sum = jnp.zeros((local_count, far_count, row_count, sample_cols), jnp.float32)
    segment = lax.all_gather(basis_half, "row", axis=1, tiled=True)
    columns = lax.slice_in_dim(far_kernel, 0, segment.shape[1], axis=3)
    mixed_rows = (
        start_sum
        + jnp.einsum("cfrw,cws->cfrs", columns, segment, preferred_element_type=jnp.float32)
    ).astype(jnp.bfloat16)
    basis_every = lax.all_gather(basis_half, "blk", axis=0, tiled=True)
    picked = jnp.take(basis_every, targets, axis=0).reshape(
        local_count, far_count, row_count, sample_cols
    )
    scale_root = jnp.sqrt(jnp.float32(full_width))
    own_samples = lax.dynamic_slice_in_dim(samples, row_offset, row_count, 1)
    parent_part = (
        jnp.einsum("crs,crt->cst", basis_half, own_samples, preferred_element_type=jnp.float32)
        / scale_root
    )
    parent_part = parent_part.reshape(local_count // 2, 2 * sample_cols, sample_cols)
    coupling_part = (
        jnp.einsum("cfrs,cfrt->cfst", picked, mixed_rows, preferred_element_type=jnp.float32)
        / scale_root
    )
    coupling, parent_samples = (
        lax.psum_scatter(coupling_part, "row", scatter_dimension=2, tiled=True),
        lax.psum_scatter(parent_part, "row", scatter_dimension=1, tiled=True),
    )
    return (basis_out, coupling, parent_samples)


def solution(mesh):
    return jax.shard_map(
        per_device,
        mesh=mesh,
        in_specs=(
            P("blk", None, "row", None),
            P("blk", None, "row", None),
            P("blk", None, None),
            P("blk", None),
        ),
        out_specs=(P("blk", "row", None), P("blk", None, "row", None), P("blk", "row", None)),
        check_vma=False,
    )
```

profile of v0, /device:TPU:1, one launch (start us, length us, event | category | flops | bytes accessed | tf_op | source)
XLA Modules:
  0.0 527.7 jit_solution(16602669929706069161)
XLA Ops:
  7.2 0.0 reduce-scatter.4.cloned.1.call-start
  7.2 0.8 eq.53
  8.1 3.7 fusion.4
  11.8 3.2 convolution_convert_fusion
  15.1 0.0 reduce-scatter.4.cloned.1.call-update
  15.1 0.0 all-reduce.2.cloned.1.call-start
  15.1 0.1 rev.3
  15.2 222.7 %reduce-scatter.4.cloned.1.call-done = bf16[8,8192]{1,0:T(8,128)(2,1)} async-done(((bf16[256,8192]{1,0:T(8,128)(2,1)}), bf16[8,8192]{1,0:T(8,128)(2,1)}) %reduce-scatter.4.cloned.1.call-update) | async-done | bytes 131088 | tf_op jit(solution)/shard_map/reduce_scatter | solution.py:34
  237.9 0.9 bitcast_convert_fusion
  238.8 0.5 fusion.21
  239.4 1.8 fusion.45
  241.2 0.0 all-reduce.2.cloned.1.call-update
  241.2 0.2 all-gather.3.cloned.1.call-start
  241.5 66.8 %all-reduce.2.cloned.1.call-done = f32[8,128,128]{2,1,0:T(8,128)} async-done(((f32[8,128,128]{2,1,0:T(8,128)}), f32[8,128,128]{2,1,0:T(8,128)}) %all-reduce.2.cloned.1.call-update) | async-done | bytes 524304 | tf_op jit(solution)/shard_map/psum | solution.py:47
  308.3 1.2 select_reduce_fusion
  309.5 1.7 fusion.17
  311.2 0.6 fusion.32
  311.8 1.7 fusion.36
  313.5 0.6 fusion.16
  314.2 0.6 fusion.47
  314.8 0.6 fusion.46
  315.5 0.6 fusion.15
  316.1 0.6 fusion.49
  316.8 0.6 fusion.48
  317.5 0.6 fusion.14
  318.1 0.6 fusion.51
  318.8 0.6 fusion.50
  319.4 0.6 fusion.13
  320.1 0.6 fusion.53
  320.7 0.6 fusion.52
  321.4 0.6 fusion.12
  322.0 0.6 fusion.55
  322.7 0.9 fusion.54
  323.6 0.6 fusion.11
  324.2 0.6 fusion.57
  324.9 0.6 fusion.56
  325.5 0.6 fusion.10
  326.2 0.6 fusion.59
  326.9 0.6 fusion.58
  327.5 0.6 fusion.9
  328.2 0.6 fusion.61
  328.8 0.6 fusion.60
  329.5 0.6 fusion.8
  330.1 0.6 fusion.63
  330.8 0.6 fusion.62
  331.4 0.6 fusion.7
  332.1 0.6 fusion.64
  332.8 0.6 fusion.65
  333.4 0.6 fusion.6
  334.1 0.6 convolution_divide_fusion
  334.7 1.6 fusion.44
  336.3 0.0 all-gather.3.cloned.1.call-update
  336.4 0.0 all-gather.5.cloned.1.call-start
  336.4 0.5 all-gather.5.cloned.1.call-update
  336.9 0.0 reduce-scatter.8.cloned.1.call-start
  337.0 0.1 reshape.83
  337.1 2.0 convolution_multiply_fusion.1
  339.1 0.0 reduce-scatter.6.cloned.1.call-start
  339.2 76.8 %all-gather.3.cloned.1.call-done = bf16[256,64,128]{2,1,0:T(8,128)(2,1)} async-done(((bf16[8,64,128]{2,1,0:T(8,128)(2,1)}), bf16[256,64,128]{2,1,0:T(8,128)(2,1)}) %all-gather.3.cloned.1.call-update) | async-done | bytes 4194320 | tf_op jit(solution)/shard_map/all_gather | solution.py:58
  416.0 2.9 gather_fusion
  419.0 25.8 %all-gather.5.cloned.1.call-done = bf16[8,512,128]{2,1,0:T(8,128)(2,1)} async-done(((bf16[8,64,128]{2,1,0:T(8,128)(2,1)}), bf16[8,512,128]{2,1,0:T(8,128)(2,1)}) %all-gather.5.cloned.1.call-update) | async-done | bytes 1048592 | tf_op jit(solution)/shard_map/all_gather | solution.py:52
  444.8 6.3 %convolution_multiply_fusion = f32[8,8,128,128]{3,2,1,0:T(8,128)} fusion(bf16[8,8,64,512]{3,2,1,0:T(8,128)(2,1)} %param.4, bf16[8,512,128]{2,1,0:T(8,128)(2,1)} %all-gather.5.cloned.1.call-done, bf16[8,8,64,128]{3,2,1,0:T(8,128)(2,1)S(1)} %bitcast.112, pred[8,8]{1,0:T(8,128)(4,1)S(1)} %compare_and_fusion), kind=kOutput, calls=%fused_computation.2 | convolution fusion | flops 673185792 | bytes 10485824 | tf_op jit(solution)/shard_map/cfrs,cfrt->cfst/dot_general | solution.py:70
  451.1 27.9 %reduce-scatter.8.cloned.1.call-done = f32[4,32,128]{2,1,0:T(8,128)} async-done(((f32[4,256,128]{2,1,0:T(8,128)}), f32[4,32,128]{2,1,0:T(8,128)}) %reduce-scatter.8.cloned.1.call-update) | async-done | bytes 65552 | tf_op jit(solution)/shard_map/reduce_scatter | solution.py:75
  479.0 41.9 %reduce-scatter.6.cloned.1.call-done = f32[8,8,16,128]{3,2,1,0:T(8,128)} async-done(((f32[8,8,128,128]{3,2,1,0:T(8,128)}), f32[8,8,16,128]{3,2,1,0:T(8,128)}) %reduce-scatter.6.cloned.1.call-update) | async-done | bytes 524304 | tf_op jit(solution)/shard_map/reduce_scatter | solution.py:74
  (15 shorter events, 0.1 us)
Async XLA Ops:
  7.2 231.7 %copy-start = (bf16[8,2,64,512]{3,2,1,0:T(8,128)(2,1)S(1)}, bf16[8,2,64,512]{3,2,1,0:T(8,128)(2,1)}, u32[]{:S(2)}) copy-start(bf16[8,2,64,512]{3,2,1,0:T(8,128)(2,1)} %param.5) | copy-start | bytes 3145732
  7.2 230.7 %reduce-scatter.4.cloned.1.call-start = ((), (), s32[]{:S(2)}) async-start(), calls=%async_computation.3 | async-start | bytes 4325376 | tf_op jit(solution)/shard_map/reduce_scatter | solution.py:34
  11.8 3.3 copy-start.1
  15.1 293.2 %all-reduce.2.cloned.1.call-start = ((), (), s32[]{:S(2)}) async-start(), calls=%async_computation.4 | async-start | bytes 1048576 | tf_op jit(solution)/shard_map/psum | solution.py:47
  241.2 174.8 %all-gather.3.cloned.1.call-start = ((), (), s32[]{:S(2)}) async-start(), calls=%async_computation.5 | async-start | bytes 4325376 | tf_op jit(solution)/shard_map/all_gather | solution.py:58
  332.1 4.9 copy-start.2
  336.4 108.5 %all-gather.5.cloned.1.call-start = ((), (), s32[]{:S(2)}) async-start(), calls=%async_computation.6 | async-start | bytes 1179648 | tf_op jit(solution)/shard_map/all_gather | solution.py:52
  336.9 142.0 %reduce-scatter.8.cloned.1.call-start = ((), (), s32[]{:S(2)}) async-start(), calls=%async_computation.8 | async-start | bytes 589824 | tf_op jit(solution)/shard_map/reduce_scatter | solution.py:75
  339.1 181.7 %reduce-scatter.6.cloned.1.call-start = ((), (), s32[]{:S(2)}) async-start(), calls=%async_computation.7 | async-start | bytes 4718592 | tf_op jit(solution)/shard_map/reduce_scatter | solution.py:74
Sparse Core Ops, SparseCore 0:
  15.2 222.6 reduce-scatter.3
  241.3 66.8 all-reduce.1
  336.5 79.5 all-gather.2
  418.3 26.4 all-gather.4
  447.8 31.1 reduce-scatter.7
  482.0 38.8 reduce-scatter.5
where the time goes:
time: 530 us; the launch traced here: 528 us
  waiting for transfers between devices  462 us (87%)
  matrix products  44.2 us (8%)
  between operations  14.5 us (3%)
    reduce_scatter x1, waiting for transfers between devices, per_device(): lax.psum_scatter(jnp.dot(onehot, products, preferred_element_type=jnp.flo...  223 us
    all_gather x1, waiting for transfers between devices, per_device(): basis_every = lax.all_gather(basis_half, 'blk', axis=0, tiled=True)  76.8 us
    psum x1, waiting for transfers between devices, per_device(): gram_mat = lax.psum(gram_part, 'row')  66.8 us
    reduce_scatter x1, waiting for transfers between devices, per_device(): lax.psum_scatter(coupling_part, 'row', scatter_dimension=2, tiled=True)  41.9 us
    reduce_scatter x1, waiting for transfers between devices, per_device(): lax.psum_scatter(parent_part, 'row', scatter_dimension=1, tiled=True)  27.9 us
    all_gather x1, waiting for transfers between devices, per_device(): segment = lax.all_gather(basis_half, 'row', axis=1, tiled=True)  25.8 us
  transfers between devices with their start and end apart: 6, of which 6 were waited for; matrix products, arithmetic and copies ran while one was open for 2% of the time, Pallas kernels for 0%

commit v1 on v0

v1 whole, which is shorter than its diff:
```python
import functools

import jax
import jax.numpy as jnp
from jax import lax
from jax.experimental import pallas as pl
from jax.experimental.pallas import tpu as pltpu
from jax.sharding import Mesh, PartitionSpec as P

ITERS = 12
SLOTS = 4
META = 8
BF16 = jnp.bfloat16
F32 = jnp.float32
SMEM_SPEC = pl.BlockSpec(memory_space=pltpu.SMEM)
BLK = ("y", "z")
ROW = ("x", "core")


def whole(shape):
    return pl.BlockSpec(shape, lambda *_: (0,) * len(shape))


def far_kernel_body(groups, target, far, near, own, sibling, send, minus_near, slot_of, count, slot_id):
    j = pl.program_id(0)
    far_count, rows, width = far.shape[1:]
    local = target.shape[0]

    @pl.when(j == 0)
    def _():
        def clear_count(i, carry):
            count[i] = 0
            return carry

        def clear_id(i, carry):
            slot_id[i] = -1
            return carry

        lax.fori_loop(0, groups, clear_count, 0)
        lax.fori_loop(0, groups * SLOTS, clear_id, 0)

        def place(b, carry):
            t = target[b // far_count, b % far_count]
            h = jnp.clip(t // local, 0, groups - 1)
            c = jnp.minimum(count[h], SLOTS - 1)
            count[h] = c + 1
            slot_of[b] = h * SLOTS + c
            slot_id[h * SLOTS + c] = t % local
            return carry

        lax.fori_loop(0, local * far_count, place, 0)
        row = lax.broadcasted_iota(jnp.int32, (META, send.shape[2]), 0)

        def header(h, carry):
            send[h, : SLOTS * rows] = jnp.zeros((SLOTS * rows, send.shape[2]), BF16)
            ids = jnp.full(row.shape, -1, jnp.int32)
            for c in range(SLOTS):
                ids = jnp.where(row == c, slot_id[h * SLOTS + c], ids)
            send[h, SLOTS * rows :] = ids.astype(F32).astype(BF16)
            return carry

        lax.fori_loop(0, groups, header, 0)

    product = jnp.dot(far[0].reshape(far_count * rows, width), own[0], preferred_element_type=F32)
    product = product.astype(BF16).reshape(far_count, rows, send.shape[2])
    for k in range(far_count):
        q = slot_of[j * far_count + k]
        start = pl.multiple_of((q % SLOTS) * rows, rows)
        send[q // SLOTS, pl.ds(start, rows)] = product[k]
    near_sum = jnp.dot(near[0, 0], own[0], preferred_element_type=F32)
    near_sum += jnp.dot(near[0, 1], sibling[0], preferred_element_type=F32)
    minus_near[0] = -near_sum


def far_products(far_kernel, near_kernel, samples, far_target, groups):
    local, far_count, rows, width = far_kernel.shape
    cols = samples.shape[2]
    depth = SLOTS * rows + META
    flops = 2 * local * (far_count + 2) * rows * width * cols
    return pl.pallas_call(
        functools.partial(far_kernel_body, groups),
        grid=(local,),
        in_specs=[
            SMEM_SPEC,
            pl.BlockSpec((1, far_count, rows, width), lambda j: (j, 0, 0, 0)),
            pl.BlockSpec((1, 2, rows, width), lambda j: (j, 0, 0, 0)),
            pl.BlockSpec((1, width, cols), lambda j: (j, 0, 0)),
            pl.BlockSpec((1, width, cols), lambda j: (j + 1 - 2 * (j % 2), 0, 0)),
        ],
        out_specs=[
            whole((groups, depth, cols)),
            pl.BlockSpec((1, rows, cols), lambda j: (j, 0, 0)),
            SMEM_SPEC,
        ],
        out_shape=[
            jax.ShapeDtypeStruct((groups, depth, cols), BF16),
            jax.ShapeDtypeStruct((local, rows, cols), F32),
            jax.ShapeDtypeStruct((local * far_count,), jnp.int32),
        ],
        scratch_shapes=[pltpu.SMEM((groups,), jnp.int32), pltpu.SMEM((groups * SLOTS,), jnp.int32)],
        cost_estimate=pl.CostEstimate(flops=flops, bytes_accessed=9000000, transcendentals=0),
        name="far_products",
    )(far_target, far_kernel, near_kernel, samples, samples)


def gather_sum_body(ids, received, minus_near, sketch, *partial):
    local, rows, cols = minus_near.shape
    for acc in partial:
        acc[...] = jnp.zeros_like(acc)

    def step(g, carry):
        for c in range(SLOTS):
            at = ids[g, c]
            at = jnp.where((at < 0) | (at >= local), local, at)
            partial[c][at] = partial[c][at] + received[g, c * rows : (c + 1) * rows].astype(F32)
        return carry

    lax.fori_loop(0, received.shape[0], step, 0)
    total = minus_near[...]
    for acc in partial:
        total = total + acc[:local]
    sketch[...] = total


def gather_sum(ids, received, minus_near):
    local, rows, cols = minus_near.shape
    return pl.pallas_call(
        gather_sum_body,
        in_specs=[SMEM_SPEC, whole(received.shape), whole(minus_near.shape)],
        out_specs=whole(minus_near.shape),
        grid=(1,),
        out_shape=jax.ShapeDtypeStruct(minus_near.shape, F32),
        scratch_shapes=[pltpu.VMEM((local + 1, rows, cols), F32)] * SLOTS,
        cost_estimate=pl.CostEstimate(flops=2000000, bytes_accessed=3000000, transcendentals=0),
        name="gather_sum",
    )(ids, received, minus_near)


def basis_body(sketch, basis, basis_half):
    highest = lax.Precision.HIGHEST
    full_width, cols = sketch.shape
    dot = functools.partial(jnp.dot, precision=highest, preferred_element_type=F32)
    values = sketch[...]
    gram = lax.dot_general(
        values, values, (((0,), (0,)), ((), ())), precision=highest, preferred_element_type=F32
    )
    identity = (
        lax.broadcasted_iota(jnp.int32, (cols, cols), 0) == lax.broadcasted_iota(jnp.int32, (cols, cols), 1)
    ).astype(F32)
    trace = jnp.sum(jnp.sum(gram * identity, axis=1, keepdims=True), axis=0, keepdims=True)
    mean_sq = trace / (full_width * cols) + 1e-6
    level = gram / (full_width * cols * mean_sq)
    root = 1.5 * identity - 0.5 * level
    level = dot(level, root)
    for _ in range(ITERS - 2):
        step = 1.5 * identity - 0.5 * dot(root, level)
        level = dot(level, step)
        root = dot(step, root)
    step = 1.5 * identity - 0.5 * dot(root, level)
    root = dot(step, root)
    result = dot(values, root / jnp.sqrt(cols * mean_sq))
    basis[...] = result
    basis_half[...] = result.astype(BF16)


def basis_of(sketch):
    return pl.pallas_call(
        basis_body,
        in_specs=[whole(sketch.shape)],
        out_specs=[whole(sketch.shape)] * 2,
        grid=(1,),
        out_shape=[jax.ShapeDtypeStruct(sketch.shape, F32), jax.ShapeDtypeStruct(sketch.shape, BF16)],
        cost_estimate=pl.CostEstimate(flops=2000000000, bytes_accessed=1000000, transcendentals=0),
        name="basis_of",
    )(sketch)


def pick_body(ids, basis, send, half):
    local, rows, cols = basis.shape
    half[:local] = basis[...].astype(BF16)
    half[local] = jnp.zeros((rows, cols), BF16)

    def step(g, carry):
        for c in range(SLOTS):
            at = ids[g, c]
            at = jnp.where((at < 0) | (at >= local), local, at)
            send[g, c * rows : (c + 1) * rows] = half[at]
        return carry

    lax.fori_loop(0, send.shape[0], step, 0)


def pick(ids, basis):
    local, rows, cols = basis.shape
    groups = ids.shape[0]
    shape = (groups, SLOTS * rows, cols)
    return pl.pallas_call(
        pick_body,
        in_specs=[SMEM_SPEC, whole(basis.shape)],
        out_specs=whole(shape),
        grid=(1,),
        out_shape=jax.ShapeDtypeStruct(shape, BF16),
        scratch_shapes=[pltpu.VMEM((local + 1, rows, cols), BF16)],
        cost_estimate=pl.CostEstimate(flops=1000000, bytes_accessed=3000000, transcendentals=0),
        name="pick",
    )(ids, basis)


def coupling_body(slot_of, place, far, segment, picked, samples, mine, other, parent, scratch):
    j = pl.program_id(0)
    far_count, rows, width = far.shape[1:]
    cols = segment.shape[2]
    x_count, _, out_rows, _ = mine.shape
    core = place[1]
    mixed = jnp.dot(far[0].reshape(far_count * rows, width), segment[0], preferred_element_type=F32)
    mixed = mixed.astype(BF16).reshape(far_count, rows, cols)
    for k in range(far_count):
        q = slot_of[j * far_count + k]
        start = pl.multiple_of((q % SLOTS) * rows, rows)
        basis_rows = picked[q // SLOTS, pl.ds(start, rows)]
        part = lax.dot_general(
            basis_rows, mixed[k], (((0,), (0,)), ((), ())), preferred_element_type=F32
        )
        part = part.reshape(x_count, 2, out_rows, cols)
        mine[:, k] = jnp.where(core == 0, part[:, 0], part[:, 1]).astype(BF16)
        other[:, k] = jnp.where(core == 0, part[:, 1], part[:, 0]).astype(BF16)
    place_in_pair = place[0] // 4

    @pl.when(j % 2 == place_in_pair)
    def _():
        scratch[...] = lax.dot_general(
            segment[0], samples[0], (((0,), (0,)), ((), ())), preferred_element_type=F32
        ) / jnp.sqrt(F32(width))
        count = parent.shape[1]
        start = pl.multiple_of((place[0] % 4) * count, count)
        parent[j // 2] = scratch[pl.ds(start, count)]


def coupling_parts(slot_of, place, far_kernel, segment, picked, samples, x_count):
    local, far_count, rows, width = far_kernel.shape
    cols = segment.shape[2]
    blocks = local * far_count
    out_rows = cols // (2 * x_count)
    parent_rows = 2 * cols // (2 * x_count)
    flops = 2 * blocks * rows * cols * (width + cols)
    part_spec = pl.BlockSpec((x_count, far_count, out_rows, cols), lambda j: (0, j, 0, 0))
    part_shape = jax.ShapeDtypeStruct((x_count, blocks, out_rows, cols), BF16)
    return pl.pallas_call(
        coupling_body,
        grid=(local,),
        in_specs=[
            SMEM_SPEC,
            SMEM_SPEC,
            pl.BlockSpec((1, far_count, rows, width), lambda j: (j, 0, 0, 0)),
            pl.BlockSpec((1, width, cols), lambda j: (j, 0, 0)),
            whole(picked.shape),
            pl.BlockSpec((1, width, cols), lambda j: (j, 0, 0)),
        ],
        out_specs=[part_spec, part_spec, whole((local // 2, parent_rows, cols))],
        out_shape=[part_shape, part_shape, jax.ShapeDtypeStruct((local // 2, parent_rows, cols), F32)],
        scratch_shapes=[pltpu.VMEM((cols, cols), F32)],
        cost_estimate=pl.CostEstimate(flops=flops, bytes_accessed=10000000, transcendentals=0),
        name="coupling_parts",
    )(slot_of, place, far_kernel, segment, picked, samples)


def per_device(far_kernel, near_kernel, samples, far_target):
    local, far_count, rows, width = far_kernel.shape
    cols = samples.shape[2]
    groups = lax.axis_size("y") * lax.axis_size("z")
    x_count = lax.axis_size("x")
    core = lax.axis_index("core")
    place = jnp.stack([lax.axis_index("x") * 2 + core, core]).astype(jnp.int32)

    send, minus_near, slot_of = far_products(far_kernel, near_kernel, samples, far_target, groups)
    received = lax.all_to_all(send, BLK, 0, 0, tiled=True)
    ids = received[:, SLOTS * rows :, 0].astype(jnp.int32)
    sketch = gather_sum(ids, received, minus_near)
    sketch = lax.all_to_all(sketch, ROW, 0, 0, tiled=True)
    basis, basis_half = basis_of(sketch.reshape(width, cols))
    basis_out = lax.all_to_all(basis.reshape(local, rows, cols), ROW, 0, 0, tiled=True)
    segment = lax.all_gather(basis_half, ROW, axis=0, tiled=True).reshape(local, width, cols)
    picked = lax.all_to_all(pick(ids, basis_out), BLK, 0, 0, tiled=True)
    mine, other, parent = coupling_parts(
        slot_of, place, far_kernel, segment, picked, samples, x_count
    )
    partner = lax.ppermute(other, "core", [(0, 1), (1, 0)])
    pair = (mine.astype(F32) + partner.astype(F32)).astype(BF16)
    parts = lax.all_to_all(pair, "x", 0, 0, tiled=True)
    coupling = jnp.sum(parts.astype(F32), axis=0) / jnp.sqrt(F32(width))
    return basis_out, coupling.reshape(local, far_count, cols // (2 * x_count), cols), parent


def solution(mesh):
    fine = Mesh(mesh.devices.reshape(4, 8, 4, 2), ("y", "z", "x", "core"))
    return jax.shard_map(
        per_device,
        mesh=fine,
        in_specs=(
            P(BLK, None, ROW, None),
            P(BLK, None, ROW, None),
            P(BLK, None, None),
            P(BLK, None),
        ),
        out_specs=(P(BLK, ROW, None), P(BLK, None, ROW, None), P(BLK, ROW, None)),
        check_vma=False,
    )
```

time: 530 us -> 220 us (0.42)
  waiting for transfers between devices: 462 us -> 50.8 us
  blocking collectives: 0 us -> 107 us
  matrix products: 44.2 us -> 0 us
  Pallas kernels: 0 us -> 34.6 us
  starting transfers between devices: 0.42 us -> 6.2 us
    reduce_scatter x3 -> x0, waiting for transfers between devices: 292 us -> none  [the longest x1 223 us: per_device(): lax.psum_scatter(jnp.dot(onehot, products, preferred_element_type=jnp.flo...]
    all_to_all x0 -> x4, blocking collectives: none -> 107 us  [the longest x1 65.1 us: per_device(): received = lax.all_to_all(send, BLK, 0, 0, tiled=True)]
    all_gather x2 -> x1, waiting for transfers between devices: 103 us -> 27.9 us  [per_device(): lax.all_gather(basis_half, ROW, axis=0, tiled=True)]
    psum x1 -> x0, waiting for transfers between devices: 66.8 us -> none  [per_device(): gram_mat = lax.psum(gram_part, 'row')]
    dot_general x42 -> x0, matrix products: 44.2 us -> none  [the longest x12 8.83 us: inverse_root(): jnp.matmul(root_mat, level_mat, precision=highest)]
    pallas_call x0 -> x5, Pallas kernels: none -> 34.6 us  [the longest x1 11.3 us: far_products(): pl.pallas_call(functools.partial(far_kernel_body, groups), grid=(local,),...]
    all_to_all x0 -> x1, waiting for transfers between devices: none -> 19.7 us  [per_device(): picked = lax.all_to_all(pick(ids, basis_out), BLK, 0, 0, tiled=True)]
  transfers between devices with their start and end apart: 6 -> 3, of which waited for: 6 -> 3; matrix products, arithmetic and copies ran while one was open for 2% -> 0% of each run, Pallas kernels for 0% -> 0%
where the time goes in v1:
time: 220 us; the launch traced here: 219 us
  blocking collectives  107 us (49%)
  waiting for transfers between devices  50.8 us (23%)
  Pallas kernels  34.6 us (16%)
  between operations  14.1 us (6%)
  starting transfers between devices  6.2 us (3%)
  other arithmetic  3.97 us (2%)
  local copies, waits for them, and re-layouts  2.5 us (1%)
    all_to_all x1, blocking collectives, per_device(): received = lax.all_to_all(send, BLK, 0, 0, tiled=True)  65.1 us
    all_gather x1, waiting for transfers between devices, per_device(): lax.all_gather(basis_half, ROW, axis=0, tiled=True)  27.9 us
    all_to_all x1, waiting for transfers between devices, per_device(): picked = lax.all_to_all(pick(ids, basis_out), BLK, 0, 0, tiled=True)  19.7 us
    all_to_all x1, blocking collectives, per_device(): parts = lax.all_to_all(pair, 'x', 0, 0, tiled=True)  17.4 us
    all_to_all x1, blocking collectives, per_device(): sketch = lax.all_to_all(sketch, ROW, 0, 0, tiled=True)  12.9 us
    all_to_all x1, blocking collectives, per_device(): lax.all_to_all(basis.reshape(local, rows, cols), ROW, 0, 0, tiled=True)  11.5 us
    pallas_call x1, Pallas kernels, far_products(): pl.pallas_call(functools.partial(far_kernel_body, groups), grid=(local,),...  11.3 us
    pallas_call x1, Pallas kernels, coupling_parts(): pl.pallas_call(coupling_body, grid=(local,), in_specs=[SMEM_SPEC, SMEM_SP...  9.73 us
  transfers between devices with their start and end apart: 3, of which 3 were waited for; matrix products, arithmetic and copies ran while one was open for 0% of the time, Pallas kernels for 0%

profile of v1, /device:TPU:1, one launch (start us, length us, event | category | flops | bytes accessed | tf_op | source)
XLA Modules:
  0.0 219.0 jit_solution(7902840904534043645)
XLA Ops:
  7.2 11.3 %far_products.1 = (bf16[32,264,128]{2,1,0:T(8,128)(2,1)}, f32[8,64,128]{2,1,0:T(8,128)}, s32[64]{0:T(128)}) custom-call(s32[8,8]{1,0:T(8,128)} %target.1, bf16[8,8,64,512]{3,2,1,0:T(8,128)(2,1)} %far.3, bf16[8,2,64,512]{3,2,1,0:T(8,128)(2,1)} %near.1, bf16[8,512,128]{2,1,0:T(8,128)(2,1)} %samples.1, bf16[8,512,128]{2,1,0:T(8,128)(2,1)} %samples.1), custom_call_target="tpu_custom_call" | custom-call | flops 671088640 | bytes 9000000 | tf_op jit(solution)/shard_map/far_products/pallas_call | solution.py:80
  18.5 65.1 %all_to_all.25.received = bf16[32,264,128]{2,1,0:T(8,128)(2,1)S(1)} all-to-all(bf16[32,264,128]{2,1,0:T(8,128)(2,1)} %get-tuple-element.11), channel_id=1, replica_groups=mesh['y'=4,'z'=8,'x'=4,'core'=2] {'y','z'}, dimensions={0} | all-to-all | bytes 4325376 | tf_op jit(solution)/shard_map/all_to_all | solution.py:276
  83.6 0.0 copy-start
  83.6 0.3 copy.10
  83.8 0.9 bitcast_convert_fusion.ids
  84.7 0.2 copy-done
  84.9 3.0 %gather_sum.1 = f32[8,64,128]{2,1,0:T(8,128)} custom-call(s32[32,8]{1,0:T(8,128)} %bitcast_convert_fusion.ids, bf16[32,264,128]{2,1,0:T(8,128)(2,1)} %copy-done, f32[8,64,128]{2,1,0:T(8,128)} %get-tuple-element.12.minus_near), custom_call_target="tpu_custom_call" | custom-call | flops 2000000 | bytes 3000000 | tf_op jit(solution)/shard_map/gather_sum/pallas_call | solution.py:127
  87.9 12.9 %all_to_all.26 = f32[8,64,128]{2,1,0:T(8,128)} all-to-all(f32[8,64,128]{2,1,0:T(8,128)} %gather_sum.1), channel_id=1, replica_groups=mesh['y'=4,'z'=8,'x'=4,'core'=2] {'x','core'}, dimensions={0} | all-to-all | bytes 524288 | tf_op jit(solution)/shard_map/all_to_all | solution.py:279
  100.9 7.8 %basis_of.1 = (f32[512,128]{1,0:T(8,128)}, bf16[512,128]{1,0:T(8,128)(2,1)}) custom-call(f32[512,128]{1,0:T(8,128)} %bitcast.11), custom_call_target="tpu_custom_call" | custom-call | flops 2000000000 | bytes 1000000 | tf_op jit(solution)/shard_map/basis_of/pallas_call | solution.py:167
  108.6 11.5 %all_to_all.27.basis = f32[8,64,128]{2,1,0:T(8,128)} all-to-all(f32[8,64,128]{2,1,0:T(8,128)} %bitcast.12), channel_id=1, replica_groups=mesh['y'=4,'z'=8,'x'=4,'core'=2] {'x','core'}, dimensions={0} | all-to-all | bytes 524288 | tf_op jit(solution)/shard_map/all_to_all | solution.py:281
  120.2 2.8 %pick.1 = bf16[32,256,128]{2,1,0:T(8,128)(2,1)} custom-call(s32[32,8]{1,0:T(8,128)} %bitcast_convert_fusion.ids, f32[8,64,128]{2,1,0:T(8,128)} %all_to_all.27.basis), custom_call_target="tpu_custom_call" | custom-call | flops 1000000 | bytes 3000000 | tf_op jit(solution)/shard_map/pick/pallas_call | solution.py:197
  122.9 4.0 %all-to-all-start.3 = ((bf16[32,256,128]{2,1,0:T(8,128)(2,1)}), bf16[32,256,128]{2,1,0:T(8,128)(2,1)S(1)}, u32[]{:S(2)}, u32[]{:S(2)}) async-start(bf16[32,256,128]{2,1,0:T(8,128)(2,1)} %pick.1), calls=%async_computation.3 | async-start | bytes 4194304 | tf_op jit(solution)/shard_map/all_to_all | solution.py:283
  126.9 0.0 all-gather.2.cloned.1.call-start
  127.0 0.7 all-gather.2.cloned.1.call-update
  127.7 0.6 pad_add_fusion.place
  128.3 27.9 %all-gather.2.cloned.1.call-done = bf16[4096,128]{1,0:T(8,128)(2,1)} async-done(((bf16[512,128]{1,0:T(8,128)(2,1)}), bf16[4096,128]{1,0:T(8,128)(2,1)}) %all-gather.2.cloned.1.call-update) | async-done | bytes 1048592 | tf_op jit(solution)/shard_map/all_gather | solution.py:282
  156.1 19.7 %all-to-all-done.3.picked = bf16[32,256,128]{2,1,0:T(8,128)(2,1)S(1)} async-done(((bf16[32,256,128]{2,1,0:T(8,128)(2,1)}), bf16[32,256,128]{2,1,0:T(8,128)(2,1)S(1)}, u32[]{:S(2)}, u32[]{:S(2)}) %all-to-all-start.3) | async-done | bytes 2097184 | tf_op jit(solution)/shard_map/all_to_all | solution.py:283
  175.9 0.0 copy-start.1
  175.9 1.3 copy-done.1
  177.2 9.7 %coupling_parts.1 = (bf16[4,64,16,128]{3,2,1,0:T(8,128)(2,1)}, bf16[4,64,16,128]{3,2,1,0:T(8,128)(2,1)}, f32[4,32,128]{2,1,0:T(8,128)}) custom-call(s32[64]{0:T(128)} %get-tuple-element.14.slot_of, s32[2]{0:T(128)} %pad_add_fusion.place, bf16[8,8,64,512]{3,2,1,0:T(8,128)(2,1)} %far.3, bf16[8,512,128]{2,1,0:T(8,128)(2,1)} %bitcast.9, ...), custom_call_target="tpu_custom_call" | custom-call | flops 671088640 | bytes 10000000 | tf_op jit(solution)/shard_map/coupling_parts/pallas_call | solution.py:248
  186.9 2.2 collective-permute-start
  189.1 2.5 %collective-permute-done = bf16[4,64,16,128]{3,2,1,0:T(8,128)(2,1)S(1)} collective-permute-done((bf16[4,64,16,128]{3,2,1,0:T(8,128)(2,1)}, bf16[4,64,16,128]{3,2,1,0:T(8,128)(2,1)S(1)}, u32[]{:S(2)}, u32[]{:S(2)}) %collective-permute-start) | collective-permute-done | bytes 1048608 | tf_op jit(solution)/shard_map/ppermute | solution.py:287
  191.6 1.5 add_convert_fusion
  193.1 0.0 copy-start.2
  193.1 17.4 %all_to_all.28 = bf16[4,64,16,128]{3,2,1,0:T(8,128)(2,1)S(1)} all-to-all(bf16[4,64,16,128]{3,2,1,0:T(8,128)(2,1)S(1)} %add_convert_fusion), channel_id=1, replica_groups=mesh['y'=4,'z'=8,'x'=4,'core'=2] {'x'}, dimensions={0} | all-to-all | bytes 2097152 | tf_op jit(solution)/shard_map/all_to_all | solution.py:289
  210.5 0.1 convert_reduce_fusion
  210.6 0.8 broadcast_multiply_fusion
  211.5 0.0 copy-done.2
  211.5 0.7 copy.12
  (1 shorter events, 0.0 us)
Async XLA Ops:
  83.6 1.3 copy-start
  122.9 53.0 %all-to-all-start.3 = ((bf16[32,256,128]{2,1,0:T(8,128)(2,1)}), bf16[32,256,128]{2,1,0:T(8,128)(2,1)S(1)}, u32[]{:S(2)}, u32[]{:S(2)}) async-start(bf16[32,256,128]{2,1,0:T(8,128)(2,1)} %pick.1), calls=%async_computation.3 | async-start | bytes 4194304 | tf_op jit(solution)/shard_map/all_to_all | solution.py:283
  126.9 29.2 %all-gather.2.cloned.1.call-start = ((), (), s32[]{:S(2)}) async-start(), calls=%async_computation.5 | async-start | bytes 1179648 | tf_op jit(solution)/shard_map/all_gather | solution.py:282
  175.9 1.3 copy-start.1
  186.9 4.6 %collective-permute-start = (bf16[4,64,16,128]{3,2,1,0:T(8,128)(2,1)}, bf16[4,64,16,128]{3,2,1,0:T(8,128)(2,1)S(1)}, u32[]{:S(2)}, u32[]{:S(2)}) collective-permute-start(bf16[4,64,16,128]{3,2,1,0:T(8,128)(2,1)} %get-tuple-element.17), channel_id=1, source_target_pairs={{0,1},{1,0},{2,3},{3,2},{4,5},{5,4},{6,7},{7,6},{8,9},{9,8},{10,11... | collective-permute-start | bytes 3145736 | tf_op jit(solution)/shard_map/ppermute | solution.py:287
  193.1 18.4 %copy-start.2 = (f32[8,64,128]{2,1,0:T(8,128)S(1)}, f32[8,64,128]{2,1,0:T(8,128)}, u32[]{:S(2)}) copy-start(f32[8,64,128]{2,1,0:T(8,128)} %all_to_all.27.basis) | copy-start | bytes 786436
Sparse Core Ops, SparseCore 0:
  130.2 25.9 all-gather.1

commit v2 on v1

v2 whole, which is shorter than its diff:
```python
import functools

import jax
import jax.numpy as jnp
from jax import lax
from jax.experimental import pallas as pl
from jax.experimental.pallas import tpu as pltpu
from jax.sharding import Mesh, PartitionSpec as P

ITERS = 12
SLOTS = 4
META = 8
BF16 = jnp.bfloat16
F32 = jnp.float32
SMEM_SPEC = pl.BlockSpec(memory_space=pltpu.SMEM)
VMEM_SPEC = pl.BlockSpec(memory_space=pltpu.VMEM)
BLK = ("y", "z")
ROW = ("x", "core")


def whole(shape):
    return pl.BlockSpec(shape, lambda *_: (0,) * len(shape))


def far_kernel_body(groups, target, far, samples, send, slot_of, count, slot_id):
    step = pl.program_id(0)
    pair, far_count, rows, width = far.shape
    cols = send.shape[2]
    local = target.shape[0]

    @pl.when(step == 0)
    def _():
        for i in range(groups):
            count[i] = 0
        for i in range(groups * SLOTS):
            slot_id[i] = -1

        def clear(h, carry):
            send[h, : SLOTS * rows] = jnp.zeros((SLOTS * rows, cols), BF16)
            return carry

        lax.fori_loop(0, groups, clear, 0)

    for i in range(pair):
        j = step * pair + i
        product = jnp.dot(far[i].reshape(far_count * rows, width), samples[i], preferred_element_type=F32)
        product = product.astype(BF16).reshape(far_count, rows, cols)
        for k in range(far_count):
            t = target[j, k]
            h = jnp.clip(t // local, 0, groups - 1)
            c = jnp.minimum(count[h], SLOTS - 1)
            count[h] = c + 1
            slot_of[j * far_count + k] = h * SLOTS + c
            slot_id[h * SLOTS + c] = t % local
            start = pl.multiple_of(c * rows, rows)
            send[h, pl.ds(start, rows)] = product[k]

    @pl.when(step == pl.num_programs(0) - 1)
    def _():
        row = lax.broadcasted_iota(jnp.int32, (META, cols), 0)

        def header(h, carry):
            ids = jnp.full(row.shape, -1, jnp.int32)
            for c in range(SLOTS):
                ids = jnp.where(row == c, slot_id[h * SLOTS + c], ids)
            send[h, SLOTS * rows :] = ids.astype(F32).astype(BF16)
            return carry

        lax.fori_loop(0, groups, header, 0, unroll=4)


def far_products(far_kernel, samples, far_target, groups):
    local, far_count, rows, width = far_kernel.shape
    cols = samples.shape[2]
    depth = SLOTS * rows + META
    pair = 2
    flops = 2 * local * far_count * rows * width * cols
    return pl.pallas_call(
        functools.partial(far_kernel_body, groups),
        grid=(local // pair,),
        in_specs=[
            SMEM_SPEC,
            pl.BlockSpec((pair, far_count, rows, width), lambda j: (j, 0, 0, 0)),
            pl.BlockSpec((pair, width, cols), lambda j: (j, 0, 0)),
        ],
        out_specs=[VMEM_SPEC, SMEM_SPEC],
        out_shape=[
            jax.ShapeDtypeStruct((groups, depth, cols), BF16),
            jax.ShapeDtypeStruct((local * far_count,), jnp.int32),
        ],
        scratch_shapes=[pltpu.SMEM((groups,), jnp.int32), pltpu.SMEM((groups * SLOTS,), jnp.int32)],
        cost_estimate=pl.CostEstimate(flops=flops, bytes_accessed=7500000, transcendentals=0),
        name="far_products",
    )(far_target, far_kernel, samples)


def near_body(near, samples, minus_near):
    for i in range(2):
        near_sum = jnp.dot(near[i, 0], samples[i], preferred_element_type=F32)
        near_sum += jnp.dot(near[i, 1], samples[1 - i], preferred_element_type=F32)
        minus_near[i] = -near_sum


def near_products(near_kernel, samples):
    local, _, rows, width = near_kernel.shape
    cols = samples.shape[2]
    return pl.pallas_call(
        near_body,
        grid=(local // 2,),
        in_specs=[
            pl.BlockSpec((2, 2, rows, width), lambda j: (j, 0, 0, 0)),
            pl.BlockSpec((2, width, cols), lambda j: (j, 0, 0)),
        ],
        out_specs=pl.BlockSpec((2, rows, cols), lambda j: (j, 0, 0)),
        out_shape=jax.ShapeDtypeStruct((local, rows, cols), F32),
        cost_estimate=pl.CostEstimate(
            flops=4 * local * rows * width * cols, bytes_accessed=2500000, transcendentals=0
        ),
        name="near_products",
    )(near_kernel, samples)


def gather_sum_body(ids, received, minus_near, sketch, *partial):
    local, rows, cols = minus_near.shape
    for acc in partial:
        acc[...] = jnp.zeros_like(acc)

    def step(g, carry):
        for c in range(SLOTS):
            at = ids[g, c]
            at = jnp.where((at < 0) | (at >= local), local, at)
            partial[c][at] = partial[c][at] + received[g, c * rows : (c + 1) * rows].astype(F32)
        return carry

    lax.fori_loop(0, received.shape[0], step, 0)
    total = minus_near[...]
    for acc in partial:
        total = total + acc[:local]
    sketch[...] = total.astype(BF16)


def gather_sum(ids, received, minus_near):
    local, rows, cols = minus_near.shape
    return pl.pallas_call(
        gather_sum_body,
        in_specs=[SMEM_SPEC, VMEM_SPEC, VMEM_SPEC],
        out_specs=VMEM_SPEC,
        out_shape=jax.ShapeDtypeStruct(minus_near.shape, BF16),
        scratch_shapes=[pltpu.VMEM((local + 1, rows, cols), F32)] * SLOTS,
        cost_estimate=pl.CostEstimate(flops=2000000, bytes_accessed=3000000, transcendentals=0),
        name="gather_sum",
    )(ids, received, minus_near)


def basis_body(sketch, basis_half):
    highest = lax.Precision.HIGHEST
    full_width, cols = sketch.shape
    dot = functools.partial(jnp.dot, precision=highest, preferred_element_type=F32)
    values = sketch[...].astype(F32)
    gram = lax.dot_general(
        values, values, (((0,), (0,)), ((), ())), precision=highest, preferred_element_type=F32
    )
    identity = (
        lax.broadcasted_iota(jnp.int32, (cols, cols), 0) == lax.broadcasted_iota(jnp.int32, (cols, cols), 1)
    ).astype(F32)
    trace = jnp.sum(jnp.sum(gram * identity, axis=1, keepdims=True), axis=0, keepdims=True)
    mean_sq = trace / (full_width * cols) + 1e-6
    level = gram / (full_width * cols * mean_sq)
    root = 1.5 * identity - 0.5 * level
    level = dot(level, root)
    for _ in range(ITERS - 2):
        step = 1.5 * identity - 0.5 * dot(root, level)
        level = dot(level, step)
        root = dot(step, root)
    step = 1.5 * identity - 0.5 * dot(root, level)
    root = dot(step, root)
    result = dot(values, root / jnp.sqrt(cols * mean_sq))
    basis_half[...] = result.astype(BF16)


def basis_of(sketch):
    return pl.pallas_call(
        basis_body,
        in_specs=[VMEM_SPEC],
        out_specs=VMEM_SPEC,
        out_shape=jax.ShapeDtypeStruct(sketch.shape, BF16),
        cost_estimate=pl.CostEstimate(flops=2000000000, bytes_accessed=1000000, transcendentals=0),
        name="basis_of",
    )(sketch)


def pick_body(ids, basis, send, basis_out):
    local, rows, _ = basis.shape

    def step(g, carry):
        for c in range(SLOTS):
            at = jnp.clip(ids[g, c], 0, local - 1)
            send[g, c * rows : (c + 1) * rows] = basis[at]
        return carry

    lax.fori_loop(0, send.shape[0], step, 0, unroll=2)
    basis_out[...] = basis[...].astype(F32)


def pick(ids, basis):
    local, rows, cols = basis.shape
    groups = ids.shape[0]
    shape = (groups, SLOTS * rows, cols)
    return pl.pallas_call(
        pick_body,
        in_specs=[SMEM_SPEC, VMEM_SPEC],
        out_specs=[VMEM_SPEC, VMEM_SPEC],
        out_shape=[jax.ShapeDtypeStruct(shape, BF16), jax.ShapeDtypeStruct(basis.shape, F32)],
        cost_estimate=pl.CostEstimate(flops=1000000, bytes_accessed=3000000, transcendentals=0),
        name="pick",
    )(ids, basis)


def coupling_body(slot_of, place, far, own, across, picked, samples, mine, other, parent, scratch):
    j = pl.program_id(0)
    far_count, rows, width = far.shape[1:]
    cols = own.shape[2]
    x_count, _, out_rows, _ = mine.shape
    core = place[1]
    segment = jnp.where(j % 2 == core, own[0], across[0])
    mixed = jnp.dot(far[0].reshape(far_count * rows, width), segment, preferred_element_type=F32)
    mixed = mixed.astype(BF16).reshape(far_count, rows, cols)
    zero = jnp.zeros((rows, cols), BF16)
    for k in range(0, far_count, 2):
        basis_rows = []
        for i in range(2):
            q = slot_of[j * far_count + k + i]
            start = pl.multiple_of((q % SLOTS) * rows, rows)
            basis_rows.append(picked[q // SLOTS, pl.ds(start, rows)])
        right = jnp.concatenate(
            [
                jnp.concatenate([mixed[k], zero], axis=1),
                jnp.concatenate([zero, mixed[k + 1]], axis=1),
            ],
            axis=0,
        )
        both = lax.dot_general(
            jnp.concatenate(basis_rows, axis=0),
            right,
            (((0,), (0,)), ((), ())),
            preferred_element_type=F32,
        )
        for i in range(2):
            part = both[:, i * cols : (i + 1) * cols].reshape(x_count, 2, out_rows, cols)
            mine[:, k + i] = jnp.where(core == 0, part[:, 0], part[:, 1]).astype(BF16)
            other[:, k + i] = jnp.where(core == 0, part[:, 1], part[:, 0]).astype(BF16)

    @pl.when(j % 2 == place[0] // 4)
    def _():
        scratch[...] = lax.dot_general(
            segment, samples[0], (((0,), (0,)), ((), ())), preferred_element_type=F32
        ) / jnp.sqrt(F32(width))
        count = parent.shape[1]
        start = pl.multiple_of((place[0] % 4) * count, count)
        parent[j // 2] = scratch[pl.ds(start, count)]


def coupling_parts(slot_of, place, far_kernel, own, across, picked, samples):
    local, far_count, rows, width = far_kernel.shape
    x_count, _, cols = own.shape
    blocks = local * far_count
    out_rows = cols // local
    parent_rows = 2 * cols // local
    flops = 2 * blocks * rows * cols * (width + cols)
    part_spec = pl.BlockSpec((x_count, far_count, out_rows, cols), lambda j, *_: (0, j, 0, 0))
    part_shape = jax.ShapeDtypeStruct((x_count, blocks, out_rows, cols), BF16)
    side = pl.BlockSpec(
        (1, width, cols), lambda j, slots, place: ((place[0] // 2 + x_count - j // 2) % x_count, 0, 0)
    )
    return pl.pallas_call(
        coupling_body,
        grid_spec=pltpu.PrefetchScalarGridSpec(
            num_scalar_prefetch=2,
            grid=(local,),
            in_specs=[
                pl.BlockSpec((1, far_count, rows, width), lambda j, *_: (j, 0, 0, 0)),
                side,
                side,
                VMEM_SPEC,
                pl.BlockSpec((1, width, cols), lambda j, *_: (j, 0, 0)),
            ],
            out_specs=[part_spec, part_spec, VMEM_SPEC],
            scratch_shapes=[pltpu.VMEM((cols, cols), F32)],
        ),
        out_shape=[part_shape, part_shape, jax.ShapeDtypeStruct((local // 2, parent_rows, cols), F32)],
        cost_estimate=pl.CostEstimate(flops=flops, bytes_accessed=10000000, transcendentals=0),
        name="coupling_parts",
    )(slot_of, place, far_kernel, own, across, picked, samples)


def per_device(far_kernel, near_kernel, samples, far_target):
    local, far_count, rows, width = far_kernel.shape
    cols = samples.shape[2]
    groups = lax.axis_size("y") * lax.axis_size("z")
    x_count = lax.axis_size("x")
    core = lax.axis_index("core")
    place = jnp.stack([lax.axis_index("x") * 2 + core, core]).astype(jnp.int32)

    send, slot_of = far_products(far_kernel, samples, far_target, groups)
    received = lax.all_to_all(send, BLK, 0, 0, tiled=True)
    minus_near = near_products(near_kernel, samples)
    ids = received[:, SLOTS * rows :, 0].astype(jnp.int32)
    received = pltpu.with_memory_space_constraint(received, pltpu.VMEM)
    sketch = gather_sum(ids, received, minus_near)
    sketch = lax.all_to_all(sketch, ROW, 0, 0, tiled=True)
    basis = basis_of(sketch.reshape(width, cols))
    basis_rows = lax.all_to_all(basis.reshape(local, rows, cols), ROW, 0, 0, tiled=True)
    send_rows, basis_out = pick(ids, basis_rows)
    picked = lax.all_to_all(send_rows, BLK, 0, 0, tiled=True)
    picked = pltpu.with_memory_space_constraint(picked, pltpu.VMEM)
    shifted = [
        lax.ppermute(basis, "x", [(i, (i + d) % x_count) for i in range(x_count)]) for d in range(1, x_count)
    ]
    own = jnp.stack([basis] + shifted)
    across = lax.ppermute(own, "core", [(0, 1), (1, 0)])
    mine, other, parent = coupling_parts(slot_of, place, far_kernel, own, across, picked, samples)
    partner = lax.ppermute(other, "core", [(0, 1), (1, 0)])
    pair = (mine.astype(F32) + partner.astype(F32)).astype(BF16)
    parts = lax.all_to_all(pair, "x", 0, 0, tiled=True)
    coupling = jnp.sum(parts.astype(F32), axis=0) / jnp.sqrt(F32(width))
    return basis_out, coupling.reshape(local, far_count, cols // (2 * x_count), cols), parent


def solution(mesh):
    fine = Mesh(mesh.devices.reshape(4, 8, 4, 2), ("y", "z", "x", "core"))
    return jax.shard_map(
        per_device,
        mesh=fine,
        in_specs=(
            P(BLK, None, ROW, None),
            P(BLK, None, ROW, None),
            P(BLK, None, None),
            P(BLK, None),
        ),
        out_specs=(P(BLK, ROW, None), P(BLK, None, ROW, None), P(BLK, ROW, None)),
        check_vma=False,
    )
```

time: 220 us -> 194 us (0.88)
  blocking collectives: 107 us -> 39.2 us
  waiting for transfers between devices: 50.8 us -> 93.3 us
  starting transfers between devices: 6.2 us -> 24 us
  between operations: 14.1 us -> 0.69 us
  local copies, waits for them, and re-layouts: 2.5 us -> 0.27 us
  Pallas kernels: 34.6 us -> 32.4 us
    all_to_all x1 -> x0, blocking collectives: 65.1 us -> none  [per_device(): received = lax.all_to_all(send, BLK, 0, 0, tiled=True)]
    all_to_all x1 -> x2, waiting for transfers between devices: 19.7 us -> 82.3 us  [the longest x1 46.3 us: per_device(): received = lax.all_to_all(send, BLK, 0, 0, tiled=True)]
    all_gather x1 -> x0, waiting for transfers between devices: 27.9 us -> none  [per_device(): lax.all_gather(basis_half, ROW, axis=0, tiled=True)]
    all_to_all x1 -> x2, starting transfers between devices: 4.01 us -> 18.1 us  [the longest x1 12 us: per_device(): received = lax.all_to_all(send, BLK, 0, 0, tiled=True)]
    ppermute x0 -> x4, waiting for transfers between devices: none -> 8.54 us  [the longest x3 7.56 us: per_device(): lax.ppermute(basis, 'x', [(i, (i + d) % x_count) for i in range(x_count)])]
    ppermute x0 -> x4, starting transfers between devices: none -> 3.71 us  [the longest x3 2.16 us: per_device(): lax.ppermute(basis, 'x', [(i, (i + d) % x_count) for i in range(x_count)])]
    unnamed x8 -> x7, local copies, waits for them, and re-layouts: 2.5 us -> 0.27 us
    pallas_call x5 -> x6, Pallas kernels: 34.6 us -> 32.4 us  [the longest x1 9.9 us: coupling_parts(): pl.pallas_call(coupling_body, grid_spec=pltpu.PrefetchScalarGridSpec(num_...]
  transfers between devices with their start and end apart: 3 -> 7, of which waited for: 3 -> 7; matrix products, arithmetic and copies ran while one was open for 0% -> 0% of each run, Pallas kernels for 0% -> 2%
where the time goes in v2:
time: 194 us
  waiting for transfers between devices  93.3 us (48%)
  blocking collectives  39.2 us (20%)
  Pallas kernels  32.4 us (17%)
  starting transfers between devices  24 us (12%)
  other arithmetic  3.74 us (2%)
    all_to_all x1, waiting for transfers between devices, per_device(): received = lax.all_to_all(send, BLK, 0, 0, tiled=True)  46.3 us
    all_to_all x1, waiting for transfers between devices, per_device(): picked = lax.all_to_all(send_rows, BLK, 0, 0, tiled=True)  36 us
    all_to_all x1, blocking collectives, per_device(): parts = lax.all_to_all(pair, 'x', 0, 0, tiled=True)  17.2 us
    all_to_all x1, starting transfers between devices, per_device(): received = lax.all_to_all(send, BLK, 0, 0, tiled=True)  12 us
    all_to_all x1, blocking collectives, per_device(): sketch = lax.all_to_all(sketch, ROW, 0, 0, tiled=True)  11.9 us
    all_to_all x1, blocking collectives, per_device(): lax.all_to_all(basis.reshape(local, rows, cols), ROW, 0, 0, tiled=True)  10.1 us
    pallas_call x1, Pallas kernels, coupling_parts(): pl.pallas_call(coupling_body, grid_spec=pltpu.PrefetchScalarGridSpec(num_...  9.9 us
    pallas_call x1, Pallas kernels, basis_of(): pl.pallas_call(basis_body, in_specs=[VMEM_SPEC], out_specs=VMEM_SPEC, out...  7.63 us
  transfers between devices with their start and end apart: 7, of which 7 were waited for; matrix products, arithmetic and copies ran while one was open for 0% of the time, Pallas kernels for 2%

profile of v2, /device:TPU:1, one launch (start us, length us, event | category | flops | bytes accessed | tf_op | source)
XLA Modules:
  0.0 193.6 jit_solution(6883716658500570756)
XLA Ops:
  0.6 6.0 %far_products.1 = (bf16[32,264,128]{2,1,0:T(8,128)(2,1)}, s32[64]{0:T(128)}) custom-call(s32[8,8]{1,0:T(8,128)} %target.1, bf16[8,8,64,512]{3,2,1,0:T(8,128)(2,1)} %far.3, bf16[8,512,128]{2,1,0:T(8,128)(2,1)} %samples.5), custom_call_target="tpu_custom_call" | custom-call | flops 536870912 | bytes 7500000 | tf_op jit(solution)/shard_map/far_products/pallas_call | solution.py:78
  6.7 12.0 %all-to-all-start = ((bf16[32,264,128]{2,1,0:T(8,128)(2,1)}), bf16[32,264,128]{2,1,0:T(8,128)(2,1)S(1)}, u32[]{:S(2)}, u32[]{:S(2)}) async-start(bf16[32,264,128]{2,1,0:T(8,128)(2,1)} %get-tuple-element.10), calls=%async_computation | async-start | bytes 4325376 | tf_op jit(solution)/shard_map/all_to_all | solution.py:305
  18.7 3.8 %near_products.1.minus_near = f32[8,64,128]{2,1,0:T(8,128)} custom-call(bf16[8,2,64,512]{3,2,1,0:T(8,128)(2,1)} %near.1, bf16[8,512,128]{2,1,0:T(8,128)(2,1)} %samples.5), custom_call_target="tpu_custom_call" | custom-call | flops 134217728 | bytes 2500000 | tf_op jit(solution)/shard_map/near_products/pallas_call | solution.py:107
  22.5 46.3 %all-to-all-done.received = bf16[32,264,128]{2,1,0:T(8,128)(2,1)S(1)} async-done(((bf16[32,264,128]{2,1,0:T(8,128)(2,1)}), bf16[32,264,128]{2,1,0:T(8,128)(2,1)S(1)}, u32[]{:S(2)}, u32[]{:S(2)}) %all-to-all-start) | async-done | bytes 2162720 | tf_op jit(solution)/shard_map/all_to_all | solution.py:305
  68.8 0.3 copy.10
  69.1 0.6 bitcast_convert_fusion.ids
  69.7 2.3 %gather_sum.1 = bf16[8,64,128]{2,1,0:T(8,128)(2,1)} custom-call(s32[32,8]{1,0:T(8,128)} %bitcast_convert_fusion.ids, bf16[32,264,128]{2,1,0:T(8,128)(2,1)S(1)} %all-to-all-done.received, f32[8,64,128]{2,1,0:T(8,128)} %near_products.1.minus_near), custom_call_target="tpu_custom_call" | custom-call | flops 2000000 | bytes 3000000 | tf_op jit(solution)/shard_map/gather_sum/pallas_call | solution.py:144
  72.0 11.9 %all_to_all.25 = bf16[8,64,128]{2,1,0:T(8,128)(2,1)} all-to-all(bf16[8,64,128]{2,1,0:T(8,128)(2,1)} %gather_sum.1), channel_id=1, replica_groups=mesh['y'=4,'z'=8,'x'=4,'core'=2] {'x','core'}, dimensions={0} | all-to-all | bytes 262144 | tf_op jit(solution)/shard_map/all_to_all | solution.py:310
  83.9 7.6 %basis_of.1 = bf16[512,128]{1,0:T(8,128)(2,1)} custom-call(bf16[512,128]{1,0:T(8,128)(2,1)} %bitcast.15), custom_call_target="tpu_custom_call" | custom-call | flops 2000000000 | bytes 1000000 | tf_op jit(solution)/shard_map/basis_of/pallas_call | solution.py:182
  91.5 10.1 %all_to_all.26.basis = bf16[8,64,128]{2,1,0:T(8,128)(2,1)} all-to-all(bf16[8,64,128]{2,1,0:T(8,128)(2,1)} %bitcast.13), channel_id=1, replica_groups=mesh['y'=4,'z'=8,'x'=4,'core'=2] {'x','core'}, dimensions={0} | all-to-all | bytes 262144 | tf_op jit(solution)/shard_map/all_to_all | solution.py:312
  101.6 2.7 %pick.1 = (bf16[32,256,128]{2,1,0:T(8,128)(2,1)}, f32[8,64,128]{2,1,0:T(8,128)}) custom-call(s32[32,8]{1,0:T(8,128)} %bitcast_convert_fusion.ids, bf16[8,64,128]{2,1,0:T(8,128)(2,1)} %all_to_all.26.basis), custom_call_target="tpu_custom_call" | custom-call | flops 1000000 | bytes 3000000 | tf_op jit(solution)/shard_map/pick/pallas_call | solution.py:209
  104.3 0.0 copy-start.2
  104.3 6.0 %all-to-all-start.3 = ((bf16[32,256,128]{2,1,0:T(8,128)(2,1)}), bf16[32,256,128]{2,1,0:T(8,128)(2,1)S(1)}, u32[]{:S(2)}, u32[]{:S(2)}) async-start(bf16[32,256,128]{2,1,0:T(8,128)(2,1)} %get-tuple-element.13), calls=%async_computation.3 | async-start | bytes 4194304 | tf_op jit(solution)/shard_map/all_to_all | solution.py:314
  110.3 0.0 copy-done.2
  110.4 1.0 collective-permute-start.2
  111.3 1.2 collective-permute-start.1
  112.5 0.0 collective-permute-start
  112.5 2.0 %collective-permute-done.2 = bf16[512,128]{1,0:T(8,128)(2,1)S(1)} collective-permute-done((bf16[512,128]{1,0:T(8,128)(2,1)S(1)}, bf16[512,128]{1,0:T(8,128)(2,1)S(1)}, u32[]{:S(2)}, u32[]{:S(2)}) %collective-permute-start.2) | collective-permute-done | bytes 131104 | tf_op jit(solution)/shard_map/ppermute | solution.py:317
  114.5 2.4 %collective-permute-done.1 = bf16[512,128]{1,0:T(8,128)(2,1)S(1)} collective-permute-done((bf16[512,128]{1,0:T(8,128)(2,1)S(1)}, bf16[512,128]{1,0:T(8,128)(2,1)S(1)}, u32[]{:S(2)}, u32[]{:S(2)}) %collective-permute-start.1) | collective-permute-done | bytes 131104 | tf_op jit(solution)/shard_map/ppermute | solution.py:317
  116.9 3.1 %collective-permute-done = bf16[512,128]{1,0:T(8,128)(2,1)S(1)} collective-permute-done((bf16[512,128]{1,0:T(8,128)(2,1)S(1)}, bf16[512,128]{1,0:T(8,128)(2,1)S(1)}, u32[]{:S(2)}, u32[]{:S(2)}) %collective-permute-start) | collective-permute-done | bytes 131104 | tf_op jit(solution)/shard_map/ppermute | solution.py:317
  120.1 0.1 pad_maximum_fusion.own
  120.1 0.0 copy-start
  120.2 1.6 collective-permute-start.3
  121.7 0.6 pad_add_fusion.place
  122.3 1.0 collective-permute-done.3.across
  123.2 0.0 copy-start.1
  123.3 36.0 %all-to-all-done.3.picked = bf16[32,256,128]{2,1,0:T(8,128)(2,1)S(1)} async-done(((bf16[32,256,128]{2,1,0:T(8,128)(2,1)}), bf16[32,256,128]{2,1,0:T(8,128)(2,1)S(1)}, u32[]{:S(2)}, u32[]{:S(2)}) %all-to-all-start.3) | async-done | bytes 2097184 | tf_op jit(solution)/shard_map/all_to_all | solution.py:314
  159.2 0.0 copy-done
  159.2 0.0 copy-done.1
  159.2 9.9 %coupling_parts.1 = (bf16[4,64,16,128]{3,2,1,0:T(8,128)(2,1)}, bf16[4,64,16,128]{3,2,1,0:T(8,128)(2,1)}, f32[4,32,128]{2,1,0:T(8,128)}) custom-call(s32[64]{0:T(128)} %get-tuple-element.12.slot_of, s32[2]{0:T(128)} %pad_add_fusion.place, bf16[8,8,64,512]{3,2,1,0:T(8,128)(2,1)} %far.3, bf16[4,512,128]{2,1,0:T(8,128)(2,1)} %copy-done, ...), custom_call_target="tpu_custom_call" | custom-call | flops 671088640 | bytes 10000000 | tf_op jit(solution)/shard_map/coupling_parts/pallas_call | solution.py:275
  169.1 2.2 %collective-permute-start.4 = (bf16[4,64,16,128]{3,2,1,0:T(8,128)(2,1)}, bf16[4,64,16,128]{3,2,1,0:T(8,128)(2,1)S(1)}, u32[]{:S(2)}, u32[]{:S(2)}) collective-permute-start(bf16[4,64,16,128]{3,2,1,0:T(8,128)(2,1)} %get-tuple-element.15), channel_id=1, source_target_pairs={{0,1},{1,0},{2,3},{3,2},{4,5},{5,4},{6,7},{7,6},{8,9},{9,8},{10,11... | collective-permute-start | bytes 3145736 | tf_op jit(solution)/shard_map/ppermute | solution.py:322
  171.3 2.5 %collective-permute-done.4 = bf16[4,64,16,128]{3,2,1,0:T(8,128)(2,1)S(1)} collective-permute-done((bf16[4,64,16,128]{3,2,1,0:T(8,128)(2,1)}, bf16[4,64,16,128]{3,2,1,0:T(8,128)(2,1)S(1)}, u32[]{:S(2)}, u32[]{:S(2)}) %collective-permute-start.4) | collective-permute-done | bytes 1048608 | tf_op jit(solution)/shard_map/ppermute | solution.py:322
  173.8 1.5 add_convert_fusion
  175.3 17.2 %all_to_all.27 = bf16[4,64,16,128]{3,2,1,0:T(8,128)(2,1)S(1)} all-to-all(bf16[4,64,16,128]{3,2,1,0:T(8,128)(2,1)S(1)} %add_convert_fusion), channel_id=1, replica_groups=mesh['y'=4,'z'=8,'x'=4,'core'=2] {'x'}, dimensions={0} | all-to-all | bytes 2097152 | tf_op jit(solution)/shard_map/all_to_all | solution.py:324
  192.6 0.1 convert_reduce_fusion
  192.7 0.8 broadcast_multiply_fusion
  (1 shorter events, 0.0 us)
Async XLA Ops:
  6.7 62.2 %all-to-all-start = ((bf16[32,264,128]{2,1,0:T(8,128)(2,1)}), bf16[32,264,128]{2,1,0:T(8,128)(2,1)S(1)}, u32[]{:S(2)}, u32[]{:S(2)}) async-start(bf16[32,264,128]{2,1,0:T(8,128)(2,1)} %get-tuple-element.10), calls=%async_computation | async-start | bytes 4325376 | tf_op jit(solution)/shard_map/all_to_all | solution.py:305
  104.3 6.0 %copy-start.2 = (bf16[512,128]{1,0:T(8,128)(2,1)S(1)}, bf16[512,128]{1,0:T(8,128)(2,1)}, u32[]{:S(2)}) copy-start(bf16[512,128]{1,0:T(8,128)(2,1)} %basis_of.1) | copy-start | bytes 393220
  104.3 54.9 %all-to-all-start.3 = ((bf16[32,256,128]{2,1,0:T(8,128)(2,1)}), bf16[32,256,128]{2,1,0:T(8,128)(2,1)S(1)}, u32[]{:S(2)}, u32[]{:S(2)}) async-start(bf16[32,256,128]{2,1,0:T(8,128)(2,1)} %get-tuple-element.13), calls=%async_computation.3 | async-start | bytes 4194304 | tf_op jit(solution)/shard_map/all_to_all | solution.py:314
  110.4 4.2 %collective-permute-start.2 = (bf16[512,128]{1,0:T(8,128)(2,1)S(1)}, bf16[512,128]{1,0:T(8,128)(2,1)S(1)}, u32[]{:S(2)}, u32[]{:S(2)}) collective-permute-start(bf16[512,128]{1,0:T(8,128)(2,1)S(1)} %copy-done.2), channel_id=1, source_target_pairs={{0,6},{2,0},{4,2},{6,4},{1,7},{3,1},{5,3},{7,5},{8,14},{10,8},{12,... | collective-permute-start | bytes 393224 | tf_op jit(solution)/shard_map/ppermute | solution.py:317
  111.3 5.6 %collective-permute-start.1 = (bf16[512,128]{1,0:T(8,128)(2,1)S(1)}, bf16[512,128]{1,0:T(8,128)(2,1)S(1)}, u32[]{:S(2)}, u32[]{:S(2)}) collective-permute-start(bf16[512,128]{1,0:T(8,128)(2,1)S(1)} %copy-done.2), channel_id=1, source_target_pairs={{0,4},{2,6},{4,0},{6,2},{1,5},{3,7},{5,1},{7,3},{8,12},{10,14},{12... | collective-permute-start | bytes 393224 | tf_op jit(solution)/shard_map/ppermute | solution.py:317
  112.5 7.6 %collective-permute-start = (bf16[512,128]{1,0:T(8,128)(2,1)S(1)}, bf16[512,128]{1,0:T(8,128)(2,1)S(1)}, u32[]{:S(2)}, u32[]{:S(2)}) collective-permute-start(bf16[512,128]{1,0:T(8,128)(2,1)S(1)} %copy-done.2), channel_id=1, source_target_pairs={{0,2},{2,4},{4,6},{6,0},{1,3},{3,5},{5,7},{7,1},{8,10},{10,12},{12... | collective-permute-start | bytes 393224 | tf_op jit(solution)/shard_map/ppermute | solution.py:317
  120.1 39.1 %copy-start = (bf16[4,512,128]{2,1,0:T(8,128)(2,1)}, bf16[4,512,128]{2,1,0:T(8,128)(2,1)S(1)}, u32[]{:S(2)}) copy-start(bf16[4,512,128]{2,1,0:T(8,128)(2,1)S(1)} %pad_maximum_fusion.own) | copy-start | bytes 1572868
  120.2 3.1 %collective-permute-start.3 = (bf16[4,512,128]{2,1,0:T(8,128)(2,1)S(1)}, bf16[4,512,128]{2,1,0:T(8,128)(2,1)S(1)}, u32[]{:S(2)}, u32[]{:S(2)}) collective-permute-start(bf16[4,512,128]{2,1,0:T(8,128)(2,1)S(1)} %pad_maximum_fusion.own), channel_id=1, source_target_pairs={{0,1},{1,0},{2,3},{3,2},{4,5},{5,4},{6,7},{7,6},{8,9},{9,8},{10,11... | collective-permute-start | bytes 1572872 | tf_op jit(solution)/shard_map/ppermute | solution.py:320
  123.2 36.0 %copy-start.1 = (bf16[4,512,128]{2,1,0:T(8,128)(2,1)}, bf16[4,512,128]{2,1,0:T(8,128)(2,1)S(1)}, u32[]{:S(2)}) copy-start(bf16[4,512,128]{2,1,0:T(8,128)(2,1)S(1)} %collective-permute-done.3.across) | copy-start | bytes 1572868
  169.1 4.7 %collective-permute-start.4 = (bf16[4,64,16,128]{3,2,1,0:T(8,128)(2,1)}, bf16[4,64,16,128]{3,2,1,0:T(8,128)(2,1)S(1)}, u32[]{:S(2)}, u32[]{:S(2)}) collective-permute-start(bf16[4,64,16,128]{3,2,1,0:T(8,128)(2,1)} %get-tuple-element.15), channel_id=1, source_target_pairs={{0,1},{1,0},{2,3},{3,2},{4,5},{5,4},{6,7},{7,6},{8,9},{9,8},{10,11... | collective-permute-start | bytes 3145736 | tf_op jit(solution)/shard_map/ppermute | solution.py:322
